TPU v7x, 256 devices: a whole 4x4x8 slice. The times are simulated.
256 devices in a mesh: tm: 16 (over z, core), space: 16 (over x, y).
Axes of the slice: x: 4, y: 4, z: 8, core: 2. Of those that a mesh axis runs over, the one named last changes fastest.
Arguments:
- events: bfloat16 [256, 16, 256, 256], P('tm', 'space'), may hold values from -6 to 6
- mix_weight: float32 [9, 256], replicated, may hold values from -1.8 to 1.8
- gain_in: float32 [256], replicated, may hold values from 0.25 to 1.75
- in_weight: bfloat16 [256, 256], replicated, may hold values from -0.375 to 0.375
- out_weight: bfloat16 [256, 256], replicated, may hold values from -0.375 to 0.375
- skip_gain: float32 [256], replicated, may hold values from 0.5 to 1.5
- feedforward_norm_gain: float32 [256], replicated, may hold values from 0.25 to 1.75
- gate_weight: bfloat16 [256, 1024], replicated, may hold values from -0.375 to 0.375
- up_weight: bfloat16 [256, 1024], replicated, may hold values from -0.375 to 0.375
- down_weight: bfloat16 [1024, 256], replicated, may hold values from -0.1875 to 0.1875
- decay: float32 [256, 256], replicated, may hold values from 0.45 to 0.99995, as said below
Outputs:
- layer_out: bfloat16 [256, 16, 256, 256], P('tm', 'space')
Inputs may be any that keep to these rules, and one draw needn't show every extreme that they name: Every decay lies strictly between 0 and 1.
All inputs are finite; a program needn't handle non-finite values.
Results may differ from a plain program's by a relative error of at most 0.008.
Values may be sent and summed in bfloat16 or wider, within the bound.
No kernel may reach another device: no remote copies, remote signals or barrier semaphores. Data moves between devices by JAX's collectives and lax.ppermute only.
A program may use at most 128 MiB of HBM per device.

v0:
```python
import functools

import jax
import jax.numpy as jnp
from jax import lax
from jax.experimental import pallas as pl
from jax.experimental.pallas import tpu as pltpu
from jax.sharding import PartitionSpec as P


BH = 16
BW = 16
BCOLS = 4
EPS = 1e-05
RIM = 24
INNER = tuple(range(2, 14))
OUTER = (0, 1, 14, 15)
FRONT_BINS = 4
BACK_BINS = 4
PACK_BINS = 2
STREAMS = 4


def neighbour_pairs(count, step_of):
    lines = count // BCOLS
    offset = BCOLS // 2
    pairs = []
    for source in range(count):
        place = (source + offset) % count
        row_step, column_step = step_of(place % BCOLS)
        row = (place // BCOLS + row_step) % lines
        column = place % BCOLS + column_step
        if 0 <= column < BCOLS:
            pairs.append((source, (row * BCOLS + column - offset) % count))
    return pairs


def in_hbm(array):
    return pltpu.with_memory_space_constraint(array, pltpu.HBM)


def pack_kernel(
    _, odd, *refs
):
    streams = refs[:STREAMS]
    mix, gain, skip, in_weight, decay, near, far, first_row, last_row, held, vectors, weight, rates = refs[STREAMS:]
    bins, _, tokens, _ = streams[0].shape
    share = held.shape[0] // STREAMS
    step = pl.program_id(0)

    @pl.when(step == 0)
    def _():
        vectors[0:9, :] = mix[...]
        vectors[9:10, :] = gain[...]
        vectors[10:11, :] = skip[...]
        weight[...] = in_weight[...]
        rates[...] = decay[...]

    row = lax.broadcasted_iota(jnp.int32, (2 * BH, tokens), 0)
    token = lax.broadcasted_iota(jnp.int32, (2 * BH, tokens), 1)
    facing = jnp.where(odd[0] == 1, 0, BW - 1)
    wanted = jnp.where(row < BH, row * BW + facing, (row - BH) * BW + (BW - 1 - facing))
    pick = (token == wanted).astype(jnp.float32).astype(jnp.bfloat16)
    for k, events in enumerate(streams):
        for b in range(bins):
            at = k * share + step * bins + b
            picked = jnp.dot(pick, events[b, 0], preferred_element_type=jnp.float32).astype(jnp.bfloat16)
            held[at, 0, :, :] = events[b, 0]
            near[at] = picked[0:BH]
            far[at] = picked[BH : 2 * BH]
            first_row[at] = events[b, 0, 0:BW, :]
            last_row[at] = events[b, 0, tokens - BW : tokens, :]


def pack(where, odd, events, mix, gain, skip, in_weight, decay):
    count, _, _, width = events.shape
    bins = PACK_BINS
    steps = count // (bins * STREAMS)
    edge = jax.ShapeDtypeStruct((count, BW, width), events.dtype)
    whole = pl.BlockSpec(memory_space=pltpu.VMEM)
    return pl.pallas_call(
        pack_kernel,
        grid_spec=pltpu.PrefetchScalarGridSpec(
            num_scalar_prefetch=2,
            grid=(steps,),
            in_specs=[
                pl.BlockSpec((bins,) + events.shape[1:], lambda i, where, _, k=k: (k * steps + i, 0, 0, 0))
                for k in range(STREAMS)
            ]
            + [
                fixed(mix.shape), fixed(gain.shape), fixed(skip.shape), fixed(in_weight.shape),
                pl.BlockSpec((count, width), lambda i, where, _: (where[0], 0)),
            ],
            out_specs=[whole] * 8,
        ),
        out_shape=[edge] * 4 + [
            jax.ShapeDtypeStruct(events.shape, events.dtype),
            jax.ShapeDtypeStruct((16, width), jnp.float32),
            jax.ShapeDtypeStruct(in_weight.shape, in_weight.dtype),
            jax.ShapeDtypeStruct((count, width), jnp.float32),
        ],
        name="pack",
        compiler_params=pltpu.CompilerParams(vmem_limit_bytes=16 << 20),
    )(where, odd, *(in_hbm(x) for x in (events,) * STREAMS + (mix, gain, skip, in_weight, decay)))


def rim_kernel(odd, near, far, first_row, last_row, down, up):
    place = lax.broadcasted_iota(jnp.int32, (RIM - BW, near.shape[-1]), 0)
    for b in range(near.shape[0]):
        left, right = sided(odd, near[b], far[b])
        for row, source, target in ((BH - 1, last_row, down), (0, first_row, up)):
            ends = jnp.where(place == 0, left[row : row + 1], jnp.where(place == 1, right[row : row + 1], 0.0))
            target[b, 0:BW, :] = source[b]
            target[b, BW:RIM, :] = ends.astype(jnp.bfloat16)


def sided(odd, near, far):
    near, far = near.astype(jnp.float32), far.astype(jnp.float32)
    flag = odd[0] == 1
    return jnp.where(flag, near, far), jnp.where(flag, far, near)


def rim(odd, near, far, first_row, last_row):
    count, _, width = near.shape
    whole = pl.BlockSpec(memory_space=pltpu.VMEM)
    return pl.pallas_call(
        rim_kernel,
        in_specs=[pl.BlockSpec(memory_space=pltpu.SMEM)] + [whole] * 4,
        out_specs=[whole] * 2,
        out_shape=[jax.ShapeDtypeStruct((count, RIM, width), near.dtype)] * 2,
        name="rim",
        compiler_params=pltpu.CompilerParams(vmem_limit_bytes=4 << 20),
    )(odd, near, far, first_row, last_row)


def front_kernel(rows, outer, *refs):
    if outer:
        (odd, events, near, far, top, bottom, vectors, in_weight, decay, inner_end,
         base, drive, end, edge, sides, normed, state) = refs
    else:
        (odd, events, near, far, vectors, in_weight, decay,
         base, drive, end, edge, sides, normed, state) = refs
    step = pl.program_id(0)
    bins = events.shape[0]
    width = events.shape[-1]
    size = len(rows) * BW

    @pl.when(step == 0)
    def _():
        state[...] = jnp.zeros_like(state)

    taps = [vectors[k : k + 1, :] for k in range(9)]
    taps[4] = taps[4] + 1.0
    column = lax.broadcasted_iota(jnp.int32, (BW, width), 0)
    first, last = column == 0, column == BW - 1
    gain_row, skip_row = vectors[9:10, :], vectors[10:11, :]
    for b in range(bins):
        for side, value in enumerate(sided(odd, near[b], far[b])):
            edge[side, 8:24, :] = value
            if outer:
                edge[side, 7:8, :] = top[b, BW + side : BW + side + 1, :].astype(jnp.float32)
                edge[side, 24:25, :] = bottom[b, BW + side : BW + side + 1, :].astype(jnp.float32)
            k = 2 * side
            sides[side, :, :] = (
                taps[k] * edge[side, 7:23, :]
                + taps[3 + k] * edge[side, 8:24, :]
                + taps[6 + k] * edge[side, 9:25, :]
            )
        cells = {}

        def row_of(i, b=b, cells=cells):
            if i not in cells:
                if i < 0:
                    value = top[b, 0:BW, :]
                elif i >= BH:
                    value = bottom[b, 0:BW, :]
                else:
                    value = events[b, 0, i * BW : (i + 1) * BW, :]
                cells[i] = value.astype(jnp.float32)
            return cells[i]

        for n, i in enumerate(rows):
            up, mid, down = row_of(i - 1), row_of(i), row_of(i + 1)
            from_left = taps[0] * up + taps[3] * mid + taps[6] * down
            centre = taps[1] * up + taps[4] * mid + taps[7] * down
            from_right = taps[2] * up + taps[5] * mid + taps[8] * down
            from_left = jnp.where(first, sides[0, i : i + 1, :], pltpu.roll(from_left, 1, 0))
            from_right = jnp.where(last, sides[1, i : i + 1, :], pltpu.roll(from_right, BW - 1, 0))
            mixed = centre + from_left + from_right
            power = jnp.mean(mixed * mixed, axis=-1, keepdims=True)
            scaled = (mixed * lax.rsqrt(power + EPS) * gain_row).astype(jnp.bfloat16)
            normed[b * size + n * BW : b * size + (n + 1) * BW, :] = scaled
            base[b, n * BW : (n + 1) * BW, :] = mixed + skip_row * scaled.astype(jnp.float32)
    product = jnp.dot(normed[...], in_weight[...], preferred_element_type=jnp.float32)
    for b in range(bins):
        rate = decay[pl.ds(step * bins + b, 1), :]
        term = product[b * size : (b + 1) * size] * jnp.sqrt(1.0 - rate * rate)
        drive[b, :, :] = term
        state[...] = rate * state[...] + term

    @pl.when(step == pl.num_programs(0) - 1)
    def _():
        if outer:
            end[0 : inner_end.shape[0], :] = inner_end[...]
            end[inner_end.shape[0] :, :] = state[...].astype(jnp.bfloat16)
        else:
            end[...] = state[...].astype(jnp.bfloat16)


def fixed(shape):
    return pl.BlockSpec(shape, lambda i, *_: (0,) * len(shape))


def by_bin(shape):
    return pl.BlockSpec(shape, lambda i, *_: (i,) + (0,) * (len(shape) - 1))


def front(rows, outer, odd, events, near, far, halos, vectors, in_weight, decay, inner_end):
    count, width = events.shape[0], events.shape[-1]
    bins = FRONT_BINS
    size = len(rows) * BW
    operands = [events, near, far]
    specs = [by_bin((bins, 1, BH * BW, width)), by_bin((bins, BH, width)), by_bin((bins, BH, width))]
    for halo in halos:
        operands.append(halo)
        specs.append(by_bin((bins,) + halo.shape[1:]))
    operands += [vectors, in_weight, decay]
    specs += [fixed(vectors.shape), fixed(in_weight.shape), fixed(decay.shape)]
    end_rows = size
    if outer:
        operands.append(inner_end)
        specs.append(fixed(inner_end.shape))
        end_rows = size + inner_end.shape[0]
    return pl.pallas_call(
        functools.partial(front_kernel, rows, outer),
        grid_spec=pltpu.PrefetchScalarGridSpec(
            num_scalar_prefetch=1,
            grid=(count // bins,),
            in_specs=specs,
            out_specs=[
                by_bin((bins, size, width)),
                by_bin((bins, size, width)),
                fixed((end_rows, width)),
            ],
            scratch_shapes=[
                pltpu.VMEM((2, 32, width), jnp.float32),
                pltpu.VMEM((2, BH, width), jnp.float32),
                pltpu.VMEM((bins * size, width), jnp.bfloat16),
                pltpu.VMEM((size, width), jnp.float32),
            ],
        ),
        out_shape=[
            jax.ShapeDtypeStruct((count, size, width), jnp.float32),
            jax.ShapeDtypeStruct((count, size, width), jnp.float32),
            jax.ShapeDtypeStruct((end_rows, width), jnp.bfloat16),
        ],
        name="front_outer" if outer else "front_inner",
        compiler_params=pltpu.CompilerParams(vmem_limit_bytes=24 << 20),
        cost_estimate=pl.CostEstimate(
            flops=count * size * width * (2 * width + 40), bytes_accessed=7 << 20, transcendentals=0
        ),
    )(odd, *operands)


def back_kernel(
    _, base_in, drive_in, base_out, drive_out, entering, decay, out_weight, gain, gate, upper, lower,
    result, state, held,
):
    step = pl.program_id(0)
    bins, inner, _ = base_in.shape
    tokens = result.shape[2]

    @pl.when(step == 0)
    def _():
        state[...] = entering[...].astype(jnp.float32)

    for b in range(bins):
        rate = decay[pl.ds(step * bins + b, 1), :]
        for start, drive in ((0, drive_in), (inner, drive_out)):
            stop = start + drive.shape[1]
            value = rate * state[start:stop, :] + drive[b]
            state[start:stop, :] = value
            held[b * tokens + start : b * tokens + stop, :] = value.astype(jnp.bfloat16)
    base = jnp.concatenate(
        [ref[b] for b in range(bins) for ref in (base_in, base_out)], axis=0
    )
    rows = base.shape[0]
    width = base.shape[-1]
    split = [slice(k * rows // 2, (k + 1) * rows // 2) for k in range(2)]

    def product(left, right):
        return jnp.concatenate(
            [jnp.dot(left[part], right, preferred_element_type=jnp.float32) for part in split], axis=0
        )

    resid = base + product(held[...], out_weight[...])
    power = jnp.mean(resid * resid, axis=-1, keepdims=True)
    hidden = (resid * lax.rsqrt(power + EPS) * gain[...]).astype(jnp.bfloat16)
    total = resid
    for n in range(gate.shape[-1] // width):
        part = slice(n * width, (n + 1) * width)
        opened = 0.5 * jnp.dot(hidden, gate[:, part], preferred_element_type=jnp.float32)
        raised = jnp.dot(hidden, upper[:, part], preferred_element_type=jnp.float32)
        gated = ((opened + opened * jnp.tanh(opened)) * raised).astype(jnp.bfloat16)
        total = total + product(gated, lower[part, :])
    done = total.astype(jnp.bfloat16)
    edge = (tokens - inner) // 2
    for b in range(bins):
        at = b * tokens
        result[b, 0, edge : edge + inner, :] = done[at : at + inner]
        result[b, 0, 0:edge, :] = done[at + inner : at + inner + edge]
        result[b, 0, edge + inner :, :] = done[at + inner + edge : at + tokens]


def back(where, base_in, drive_in, base_out, drive_out, entering, decay, out_weight, gain, gate, upper, lower):
    count, inner, width = base_in.shape
    outer = base_out.shape[1]
    bins = BACK_BINS
    tokens = inner + outer
    blocks = [by_bin((bins, size, width)) for size in (inner, inner, outer, outer)]
    return pl.pallas_call(
        back_kernel,
        grid_spec=pltpu.PrefetchScalarGridSpec(
            num_scalar_prefetch=1,
            grid=(count // bins,),
            in_specs=[
                *blocks,
                fixed(entering.shape),
                pl.BlockSpec((count, width), lambda i, where: (where[0], 0)),
                fixed(out_weight.shape), fixed(gain.shape), fixed(gate.shape), fixed(upper.shape), fixed(lower.shape),
            ],
            out_specs=by_bin((bins, 1, tokens, width)),
            scratch_shapes=[
                pltpu.VMEM((tokens, width), jnp.float32),
                pltpu.VMEM((bins * tokens, width), jnp.bfloat16),
            ],
        ),
        out_shape=jax.ShapeDtypeStruct((count, 1, tokens, width), jnp.bfloat16),
        name="back",
        compiler_params=pltpu.CompilerParams(vmem_limit_bytes=32 << 20),
    )(where, base_in, drive_in, base_out, drive_out, entering, decay, out_weight, gain, gate, upper, lower)


def prefix_kernel(slots, decay, result):
    peers, _, _ = slots.shape
    bins = decay.shape[0] // peers
    before = jnp.zeros(slots.shape[1:], jnp.float32)
    for k in range(peers):
        result[k] = before.astype(jnp.bfloat16)
        rate = decay[k * bins : (k + 1) * bins, :]
        rate = rate[0:8] * rate[8:16]
        for shift in (4, 2, 1):
            rate = rate * pltpu.roll(rate, shift, 0)
        before = rate[0:1] * before + slots[k].astype(jnp.float32)


def prefix(slots, decay):
    return pl.pallas_call(
        prefix_kernel,
        in_specs=[pl.BlockSpec(memory_space=pltpu.VMEM)] * 2,
        out_specs=pl.BlockSpec(memory_space=pltpu.VMEM),
        out_shape=jax.ShapeDtypeStruct(slots.shape, slots.dtype),
        name="prefix",
        compiler_params=pltpu.CompilerParams(vmem_limit_bytes=4 << 20),
    )(slots, decay)


def local(
    events, mix_weight, gain_in, in_weight, out_weight, skip_gain, feedforward_norm_gain,
    gate_weight, up_weight, down_weight, decay,
):
    _, _, tokens_dev, width = events.shape
    count = lax.axis_size("space")
    peers = lax.axis_size("tm")
    where = lax.axis_index("tm").astype(jnp.int32).reshape(1)
    odd = ((lax.axis_index("space") + BCOLS // 2) % 2).astype(jnp.int32).reshape(1)
    gain_row, skip_row = gain_in.reshape(1, width), skip_gain.reshape(1, width)
    near_edge, far_edge, first_row, last_row, held, *shared = pack(
        where, odd, events, mix_weight, gain_row, skip_row, in_weight, decay
    )
    far = lax.ppermute(far_edge, "space", neighbour_pairs(count, lambda c: (0, 1 if c % 2 else -1)))
    near = lax.ppermute(near_edge, "space", neighbour_pairs(count, lambda c: (0, -1 if c % 2 else 1)))
    down, up = rim(odd, near, far, first_row, last_row)
    top = lax.ppermute(down, "space", neighbour_pairs(count, lambda c: (1, 0)))
    bottom = lax.ppermute(up, "space", neighbour_pairs(count, lambda c: (-1, 0)))
    base_in, drive_in, end_in = front(INNER, False, odd, held, near, far, (), *shared, None)
    base_out, drive_out, ends = front(OUTER, True, odd, held, near, far, (top, bottom), *shared, end_in)
    slots = lax.all_to_all(ends.reshape(peers, tokens_dev // peers, width), "tm", 0, 0)
    entering = lax.all_to_all(prefix(slots, decay), "tm", 0, 0).reshape(tokens_dev, width)
    return back(
        where, base_in, drive_in, base_out, drive_out, entering, decay, out_weight,
        feedforward_norm_gain.reshape(1, width), gate_weight, up_weight, down_weight,
    )


def solution(mesh):
    return jax.shard_map(
        local,
        mesh=mesh,
        in_specs=(P("tm", "space", None, None), P(), P(), P(), P(), P(), P(), P(), P(), P(), P()),
        out_specs=P("tm", "space", None, None),
        check_vma=False,
    )
```

profile of v0, /device:TPU:1, one launch (start us, length us, event | category | flops | bytes accessed | tf_op | source)
XLA Modules:
  0.0 63.9 jit_solution(17573434321610983431)
XLA Ops:
  0.0 2.0 %pack.1 = (bf16[16,16,256]{2,1,0:T(8,128)(2,1)S(1)}, bf16[16,16,256]{2,1,0:T(8,128)(2,1)S(1)}, bf16[16,16,256]{2,1,0:T(8,128)(2,1)S(1)}, bf16[16,16,256]{2,1,0:T...) custom-call(s32[1]{0:T(128)} %bitcast._, ...), custom_call_target="tpu_custom_call" | custom-call | tf_op jit(solution)/shard_map/pack/pallas_call | solution.py:81
  2.0 2.2 %collective-permute-start = (bf16[16,16,256]{2,1,0:T(8,128)(2,1)S(1)}, bf16[16,16,256]{2,1,0:T(8,128)(2,1)S(1)}, u32[]{:S(2)}, u32[]{:S(2)}) collective-permute-start(bf16[16,16,256]{2,1,0:T(8,128)(2,1)S(1)} %get-tuple-element.22), channel_id=1, source_target_pairs={{0,1},{1,0},{2,3},{3,2},{4,5},{5,4},{6,7},{7,6},{8,9},{9,8},{10,11... | collective-permute-start | bytes 393224 | tf_op jit(solution)/shard_map/ppermute | solution.py:382
  4.2 6.0 %collective-permute-start.1 = (bf16[16,16,256]{2,1,0:T(8,128)(2,1)S(1)}, bf16[16,16,256]{2,1,0:T(8,128)(2,1)S(1)}, u32[]{:S(2)}, u32[]{:S(2)}) collective-permute-start(bf16[16,16,256]{2,1,0:T(8,128)(2,1)S(1)} %get-tuple-element.23), channel_id=1, source_target_pairs={{0,15},{3,4},{4,3},{7,8},{8,7},{11,12},{12,11},{15,0},{16,31},{19,... | collective-permute-start | bytes 393224 | tf_op jit(solution)/shard_map/ppermute | solution.py:381
  10.2 0.0 collective-permute-done.refs_2_.near
  10.2 3.0 %collective-permute-done.1.refs_3_.far = bf16[16,16,256]{2,1,0:T(8,128)(2,1)S(1)} collective-permute-done((bf16[16,16,256]{2,1,0:T(8,128)(2,1)S(1)}, bf16[16,16,256]{2,1,0:T(8,128)(2,1)S(1)}, u32[]{:S(2)}, u32[]{:S(2)}) %collective-permute-start.1) | collective-permute-done | bytes 131104 | tf_op jit(solution)/shard_map/ppermute | solution.py:381
  13.2 0.1 rim.1
  13.3 0.1 collective-permute-start.2
  13.4 2.7 %collective-permute-start.3 = (bf16[16,24,256]{2,1,0:T(8,128)(2,1)S(1)}, bf16[16,24,256]{2,1,0:T(8,128)(2,1)S(1)}, u32[]{:S(2)}, u32[]{:S(2)}) collective-permute-start(bf16[16,24,256]{2,1,0:T(8,128)(2,1)S(1)} %get-tuple-element.32), channel_id=1, source_target_pairs={{0,12},{1,13},{2,14},{3,15},{4,0},{5,1},{6,2},{7,3},{8,4},{9,5},{1... | collective-permute-start | bytes 589832 | tf_op jit(solution)/shard_map/ppermute | solution.py:385
  16.0 4.3 %front_inner.1 = (f32[16,192,256]{2,1,0:T(8,128)S(1)}, f32[16,192,256]{2,1,0:T(8,128)S(1)}, bf16[192,256]{1,0:T(8,128)(2,1)S(1)}) custom-call(s32[1]{0:T(128)} %bitcast.1.odd.refs_0_, bf16[16,1,256,256]{3,2,1,0:T(8,128)(2,1)S(1)} %get-tuple-element.21.refs_1_, bf16[16,16,256]{2,1,0:T(8,128)(2,1)S(1)} %collective-permute-done.refs_2_.near, ...), custom_call_target="tpu_custom_call" | custom-call | flops 434110464 | bytes 7340032 | tf_op jit(solution)/shard_map/front_inner/pallas_call | solution.py:234
  20.3 0.0 copy-start
  20.3 0.0 copy-start.1
  20.3 0.0 copy-start.2
  20.4 0.0 copy-start.3
  20.4 0.0 copy-start.4
  20.4 0.0 copy-start.5
  20.4 0.0 collective-permute-done.2.refs_4_
  20.4 0.0 collective-permute-done.3.refs_5_
  20.4 2.2 %front_outer.1 = (f32[16,64,256]{2,1,0:T(8,128)S(1)}, f32[16,64,256]{2,1,0:T(8,128)S(1)}, bf16[256,256]{1,0:T(8,128)(2,1)S(1)}) custom-call(s32[1]{0:T(128)} %bitcast.1.odd.refs_0_, bf16[16,1,256,256]{3,2,1,0:T(8,128)(2,1)S(1)} %get-tuple-element.21.refs_1_, bf16[16,16,256]{2,1,0:T(8,128)(2,1)S(1)} %collective-permute-done.refs_2_.near, ...), custom_call_target="tpu_custom_call" | custom-call | flops 144703488 | bytes 7340032 | tf_op jit(solution)/shard_map/front_outer/pallas_call | solution.py:234
  22.7 19.8 %all_to_all.10.slots = bf16[16,16,256]{2,1,0:T(8,128)(2,1)S(1)} all-to-all(bf16[16,16,256]{2,1,0:T(8,128)(2,1)S(1)} %bitcast.8), channel_id=1, replica_groups=mesh['tm'=16,'space'=16] {'tm'}, dimensions={0} | all-to-all | bytes 262144 | tf_op jit(solution)/shard_map/all_to_all | solution.py:388
  42.5 0.0 copy-done
  42.5 0.1 prefix.1
  42.5 11.6 %all_to_all.11 = bf16[16,16,256]{2,1,0:T(8,128)(2,1)S(1)} all-to-all(bf16[16,16,256]{2,1,0:T(8,128)(2,1)S(1)} %prefix.1), channel_id=1, replica_groups=mesh['tm'=16,'space'=16] {'tm'}, dimensions={0} | all-to-all | bytes 262144 | tf_op jit(solution)/shard_map/all_to_all | solution.py:389
  54.1 0.0 copy-done.1
  54.1 0.0 copy-done.2
  54.1 0.0 copy-done.3
  54.1 0.0 copy-done.4
  54.1 0.0 copy-done.5
  54.1 9.8 %back.1 = bf16[16,1,256,256]{3,2,1,0:T(8,128)(2,1)} custom-call(s32[1]{0:T(128)} %bitcast._, f32[16,192,256]{2,1,0:T(8,128)S(1)} %get-tuple-element.27.base_in, f32[16,192,256]{2,1,0:T(8,128)S(1)} %get-tuple-element.28.drive_in, f32[16,64,256]{2,1,0:T(8,128)S(1)} %get-tuple-element.34.base_out, f32[16,64,256]{2,1,0:T(8,128)S(1)} %get-tuple-element.35.drive_out, ...), custom_call_target="tpu_custom_call" | custom-call | tf_op jit(solution)/shard_map/back/pallas_call | solution.py:321
Async XLA Ops:
  2.0 8.2 %collective-permute-start = (bf16[16,16,256]{2,1,0:T(8,128)(2,1)S(1)}, bf16[16,16,256]{2,1,0:T(8,128)(2,1)S(1)}, u32[]{:S(2)}, u32[]{:S(2)}) collective-permute-start(bf16[16,16,256]{2,1,0:T(8,128)(2,1)S(1)} %get-tuple-element.22), channel_id=1, source_target_pairs={{0,1},{1,0},{2,3},{3,2},{4,5},{5,4},{6,7},{7,6},{8,9},{9,8},{10,11... | collective-permute-start | bytes 393224 | tf_op jit(solution)/shard_map/ppermute | solution.py:382
  4.2 9.0 %collective-permute-start.1 = (bf16[16,16,256]{2,1,0:T(8,128)(2,1)S(1)}, bf16[16,16,256]{2,1,0:T(8,128)(2,1)S(1)}, u32[]{:S(2)}, u32[]{:S(2)}) collective-permute-start(bf16[16,16,256]{2,1,0:T(8,128)(2,1)S(1)} %get-tuple-element.23), channel_id=1, source_target_pairs={{0,15},{3,4},{4,3},{7,8},{8,7},{11,12},{12,11},{15,0},{16,31},{19,... | collective-permute-start | bytes 393224 | tf_op jit(solution)/shard_map/ppermute | solution.py:381
  13.3 7.1 %collective-permute-start.2 = (bf16[16,24,256]{2,1,0:T(8,128)(2,1)S(1)}, bf16[16,24,256]{2,1,0:T(8,128)(2,1)S(1)}, u32[]{:S(2)}, u32[]{:S(2)}) collective-permute-start(bf16[16,24,256]{2,1,0:T(8,128)(2,1)S(1)} %get-tuple-element.31), channel_id=1, source_target_pairs={{0,4},{1,5},{2,6},{3,7},{4,8},{5,9},{6,10},{7,11},{8,12},{9,13},{1... | collective-permute-start | bytes 589832 | tf_op jit(solution)/shard_map/ppermute | solution.py:384
  13.4 7.0 %collective-permute-start.3 = (bf16[16,24,256]{2,1,0:T(8,128)(2,1)S(1)}, bf16[16,24,256]{2,1,0:T(8,128)(2,1)S(1)}, u32[]{:S(2)}, u32[]{:S(2)}) collective-permute-start(bf16[16,24,256]{2,1,0:T(8,128)(2,1)S(1)} %get-tuple-element.32), channel_id=1, source_target_pairs={{0,12},{1,13},{2,14},{3,15},{4,0},{5,1},{6,2},{7,3},{8,4},{9,5},{1... | collective-permute-start | bytes 589832 | tf_op jit(solution)/shard_map/ppermute | solution.py:385
  20.3 22.2 %copy-start = (f32[256,256]{1,0:T(8,128)S(1)}, f32[256,256]{1,0:T(8,128)}, u32[]{:S(2)}) copy-start(f32[256,256]{1,0:T(8,128)} %decay.3) | copy-start | bytes 786436
  20.3 33.8 %copy-start.1 = (bf16[256,1024]{1,0:T(8,128)(2,1)S(1)}, bf16[256,1024]{1,0:T(8,128)(2,1)}, u32[]{:S(2)}) copy-start(bf16[256,1024]{1,0:T(8,128)(2,1)} %gate.1) | copy-start | bytes 1572868
  20.3 33.8 %copy-start.2 = (bf16[256,1024]{1,0:T(8,128)(2,1)S(1)}, bf16[256,1024]{1,0:T(8,128)(2,1)}, u32[]{:S(2)}) copy-start(bf16[256,1024]{1,0:T(8,128)(2,1)} %upper.1) | copy-start | bytes 1572868
  20.4 33.8 %copy-start.3 = (bf16[1024,256]{1,0:T(8,128)(2,1)S(1)}, bf16[1024,256]{1,0:T(8,128)(2,1)}, u32[]{:S(2)}) copy-start(bf16[1024,256]{1,0:T(8,128)(2,1)} %lower.1) | copy-start | bytes 1572868
  20.4 33.8 %copy-start.4 = (bf16[256,256]{1,0:T(8,128)(2,1)S(1)}, bf16[256,256]{1,0:T(8,128)(2,1)}, u32[]{:S(2)}) copy-start(bf16[256,256]{1,0:T(8,128)(2,1)} %out_weight.1) | copy-start | bytes 393220
  20.4 33.8 %copy-start.5 = (f32[256]{0:T(256)S(1)}, f32[256]{0:T(256)}, u32[]{:S(2)}) copy-start(f32[256]{0:T(256)} %param.17) | copy-start | bytes 3076
where the time goes:
time: 64.1 us; the launch traced here: 63.9 us
  blocking collectives  31.4 us (49%)
  Pallas kernels  18.4 us (29%)
  starting transfers between devices  10.9 us (17%)
  waiting for transfers between devices  3.02 us (5%)
    all_to_all x1, blocking collectives, local(): lax.all_to_all(ends.reshape(peers, tokens_dev // peers, width), 'tm', 0, 0)  19.8 us
    all_to_all x1, blocking collectives, local(): lax.all_to_all(prefix(slots, decay), 'tm', 0, 0).reshape(tokens_dev, width)  11.6 us
    pallas_call x1, Pallas kernels, back(): pl.pallas_call(back_kernel, grid_spec=pltpu.PrefetchScalarGridSpec(num_sc...  9.79 us
    pallas_call x2, Pallas kernels, front(): pl.pallas_call(functools.partial(front_kernel, rows, outer), grid_spec=pl...  6.51 us
    ppermute x1, starting transfers between devices, local(): lax.ppermute(far_edge, 'space', neighbour_pairs(count, lambda c: (0, 1 if...  5.99 us
    ppermute x1, waiting for transfers between devices, local(): lax.ppermute(far_edge, 'space', neighbour_pairs(count, lambda c: (0, 1 if...  3.01 us
    ppermute x1, starting transfers between devices, local(): lax.ppermute(up, 'space', neighbour_pairs(count, lambda c: (-1, 0)))  2.66 us
    ppermute x1, starting transfers between devices, local(): lax.ppermute(near_edge, 'space', neighbour_pairs(count, lambda c: (0, -1...  2.2 us
  transfers between devices with their start and end apart: 4, of which 1 were waited for; matrix products, arithmetic and copies ran while one was open for 0% of the time, Pallas kernels for 7%

commit v1 on v0

--- a/solution.py
+++ b/solution.py
@@ -13,9 +13,9 @@
 BCOLS = 4
 EPS = 1e-05
 RIM = 24
-INNER = tuple(range(2, 14))
-OUTER = (0, 1, 14, 15)
-FRONT_BINS = 4
+INNER = tuple(range(1, 15))
+OUTER = (0, 15)
+FRONT_BINS = 8
 BACK_BINS = 4
 PACK_BINS = 2
 STREAMS = 4
@@ -43,8 +43,8 @@
     _, odd, *refs
 ):
     streams = refs[:STREAMS]
-    mix, gain, skip, in_weight, decay, near, far, first_row, last_row, held, vectors, weight, rates = refs[STREAMS:]
-    bins, _, tokens, _ = streams[0].shape
+    mix, gain, in_weight, decay, near, far, first_row, last_row, held, vectors, weight, rates = refs[STREAMS:]
+    bins, _, tokens, width = streams[0].shape
     share = held.shape[0] // STREAMS
     step = pl.program_id(0)
 
@@ -52,9 +52,16 @@
     def _():
         vectors[0:9, :] = mix[...]
         vectors[9:10, :] = gain[...]
-        vectors[10:11, :] = skip[...]
         weight[...] = in_weight[...]
-        rates[...] = decay[...]
+        rate = decay[...]
+        count = rate.shape[0]
+        scale = jnp.sqrt(1.0 - rate * rate)
+        rates[0:count, :] = rate
+        rates[count : 2 * count, :] = scale
+        tail = jnp.ones((1, width), jnp.float32)
+        for t in reversed(range(count)):
+            rates[2 * count + t : 2 * count + t + 1, :] = scale[t : t + 1] * tail
+            tail = tail * rate[t : t + 1]
 
     row = lax.broadcasted_iota(jnp.int32, (2 * BH, tokens), 0)
     token = lax.broadcasted_iota(jnp.int32, (2 * BH, tokens), 1)
@@ -72,7 +79,7 @@
             last_row[at] = events[b, 0, tokens - BW : tokens, :]
 
 
-def pack(where, odd, events, mix, gain, skip, in_weight, decay):
+def pack(where, odd, events, mix, gain, in_weight, decay):
     count, _, _, width = events.shape
     bins = PACK_BINS
     steps = count // (bins * STREAMS)
@@ -88,7 +95,7 @@
                 for k in range(STREAMS)
             ]
             + [
-                fixed(mix.shape), fixed(gain.shape), fixed(skip.shape), fixed(in_weight.shape),
+                fixed(mix.shape), fixed(gain.shape), fixed(in_weight.shape),
                 pl.BlockSpec((count, width), lambda i, where, _: (where[0], 0)),
             ],
             out_specs=[whole] * 8,
@@ -97,11 +104,11 @@
             jax.ShapeDtypeStruct(events.shape, events.dtype),
             jax.ShapeDtypeStruct((16, width), jnp.float32),
             jax.ShapeDtypeStruct(in_weight.shape, in_weight.dtype),
-            jax.ShapeDtypeStruct((count, width), jnp.float32),
+            jax.ShapeDtypeStruct((3 * count, width), jnp.float32),
         ],
         name="pack",
         compiler_params=pltpu.CompilerParams(vmem_limit_bytes=16 << 20),
-    )(where, odd, *(in_hbm(x) for x in (events,) * STREAMS + (mix, gain, skip, in_weight, decay)))
+    )(where, odd, *(in_hbm(x) for x in (events,) * STREAMS + (mix, gain, in_weight, decay)))
 
 
 def rim_kernel(odd, near, far, first_row, last_row, down, up):
@@ -135,13 +142,13 @@
 
 def front_kernel(rows, outer, *refs):
     if outer:
-        (odd, events, near, far, top, bottom, vectors, in_weight, decay, inner_end,
-         base, drive, end, edge, sides, normed, state) = refs
+        (odd, events, near, far, top, bottom, vectors, in_weight, rates, inner_end,
+         mixture, normed, drive, end, edge, sides, state) = refs
     else:
-        (odd, events, near, far, vectors, in_weight, decay,
-         base, drive, end, edge, sides, normed, state) = refs
+        (odd, events, near, far, vectors, in_weight, rates,
+         mixture, normed, drive, end, edge, sides, state) = refs
     step = pl.program_id(0)
-    bins = events.shape[0]
+    bins = events.shape[0] if outer else FRONT_BINS
     width = events.shape[-1]
     size = len(rows) * BW
 
@@ -151,15 +158,17 @@
 
     taps = [vectors[k : k + 1, :] for k in range(9)]
     taps[4] = taps[4] + 1.0
-    column = lax.broadcasted_iota(jnp.int32, (BW, width), 0)
-    first, last = column == 0, column == BW - 1
-    gain_row, skip_row = vectors[9:10, :], vectors[10:11, :]
+    column = lax.broadcasted_iota(jnp.int32, (BW // 2, width), 0)
+    first, last = column == 0, column == BW // 2 - 1
+    gain_row = vectors[9:10, :]
+    count = events.shape[0]
     for b in range(bins):
-        for side, value in enumerate(sided(odd, near[b], far[b])):
+        at = step * bins + b
+        for side, value in enumerate(sided(odd, near[at], far[at])):
             edge[side, 8:24, :] = value
             if outer:
-                edge[side, 7:8, :] = top[b, BW + side : BW + side + 1, :].astype(jnp.float32)
-                edge[side, 24:25, :] = bottom[b, BW + side : BW + side + 1, :].astype(jnp.float32)
+                edge[side, 7:8, :] = top[at, BW + side : BW + side + 1, :].astype(jnp.float32)
+                edge[side, 24:25, :] = bottom[at, BW + side : BW + side + 1, :].astype(jnp.float32)
             k = 2 * side
             sides[side, :, :] = (
                 taps[k] * edge[side, 7:23, :]
@@ -168,14 +177,14 @@
             )
         cells = {}
 
-        def row_of(i, b=b, cells=cells):
+        def row_of(i, at=at, cells=cells):
             if i not in cells:
                 if i < 0:
-                    value = top[b, 0:BW, :]
+                    value = top[at, 0:BW, :]
                 elif i >= BH:
-                    value = bottom[b, 0:BW, :]
+                    value = bottom[at, 0:BW, :]
                 else:
-                    value = events[b, 0, i * BW : (i + 1) * BW, :]
+                    value = events[at, 0, i * BW : (i + 1) * BW, :]
                 cells[i] = value.astype(jnp.float32)
             return cells[i]
 
@@ -184,19 +193,28 @@
             from_left = taps[0] * up + taps[3] * mid + taps[6] * down
             centre = taps[1] * up + taps[4] * mid + taps[7] * down
             from_right = taps[2] * up + taps[5] * mid + taps[8] * down
-            from_left = jnp.where(first, sides[0, i : i + 1, :], pltpu.roll(from_left, 1, 0))
-            from_right = jnp.where(last, sides[1, i : i + 1, :], pltpu.roll(from_right, BW - 1, 0))
+            low = pltpu.roll(from_left[: BW // 2], 1, 0)
+            high = pltpu.roll(from_left[BW // 2 :], 1, 0)
+            from_left = jnp.concatenate(
+                [jnp.where(first, sides[0, i : i + 1, :], low), jnp.where(first, low, high)], axis=0
+            )
+            low = pltpu.roll(from_right[: BW // 2], BW // 2 - 1, 0)
+            high = pltpu.roll(from_right[BW // 2 :], BW // 2 - 1, 0)
+            from_right = jnp.concatenate(
+                [jnp.where(last, high, low), jnp.where(last, sides[1, i : i + 1, :], high)], axis=0
+            )
             mixed = centre + from_left + from_right
             power = jnp.mean(mixed * mixed, axis=-1, keepdims=True)
-            scaled = (mixed * lax.rsqrt(power + EPS) * gain_row).astype(jnp.bfloat16)
-            normed[b * size + n * BW : b * size + (n + 1) * BW, :] = scaled
-            base[b, n * BW : (n + 1) * BW, :] = mixed + skip_row * scaled.astype(jnp.float32)
-    product = jnp.dot(normed[...], in_weight[...], preferred_element_type=jnp.float32)
+            mixture[at, n * BW : (n + 1) * BW, :] = mixed
+            normed[at, n * BW : (n + 1) * BW, :] = (mixed * lax.rsqrt(power + EPS) * gain_row).astype(jnp.bfloat16)
+    rows_now = normed[pl.ds(step * bins, bins)].reshape(bins * size, width)
+    product = jnp.dot(rows_now, in_weight[...], preferred_element_type=jnp.float32)
+    total = state[...]
     for b in range(bins):
-        rate = decay[pl.ds(step * bins + b, 1), :]
-        term = product[b * size : (b + 1) * size] * jnp.sqrt(1.0 - rate * rate)
-        drive[b, :, :] = term
-        state[...] = rate * state[...] + term
+        term = product[b * size : (b + 1) * size]
+        drive[step * bins + b, :, :] = term
+        total = total + rates[pl.ds(2 * count + step * bins + b, 1), :] * term
+    state[...] = total
 
     @pl.when(step == pl.num_programs(0) - 1)
     def _():
@@ -217,40 +235,30 @@
 
 def front(rows, outer, odd, events, near, far, halos, vectors, in_weight, decay, inner_end):
     count, width = events.shape[0], events.shape[-1]
-    bins = FRONT_BINS
+    bins = count if outer else FRONT_BINS
     size = len(rows) * BW
-    operands = [events, near, far]
-    specs = [by_bin((bins, 1, BH * BW, width)), by_bin((bins, BH, width)), by_bin((bins, BH, width))]
-    for halo in halos:
-        operands.append(halo)
-        specs.append(by_bin((bins,) + halo.shape[1:]))
-    operands += [vectors, in_weight, decay]
-    specs += [fixed(vectors.shape), fixed(in_weight.shape), fixed(decay.shape)]
+    whole = pl.BlockSpec(memory_space=pltpu.VMEM)
+    operands = [events, near, far, *halos, vectors, in_weight, decay]
     end_rows = size
     if outer:
         operands.append(inner_end)
-        specs.append(fixed(inner_end.shape))
         end_rows = size + inner_end.shape[0]
     return pl.pallas_call(
         functools.partial(front_kernel, rows, outer),
         grid_spec=pltpu.PrefetchScalarGridSpec(
             num_scalar_prefetch=1,
             grid=(count // bins,),
-            in_specs=specs,
-            out_specs=[
-                by_bin((bins, size, width)),
-                by_bin((bins, size, width)),
-                fixed((end_rows, width)),
-            ],
+            in_specs=[whole] * len(operands),
+            out_specs=[whole] * 4,
             scratch_shapes=[
                 pltpu.VMEM((2, 32, width), jnp.float32),
                 pltpu.VMEM((2, BH, width), jnp.float32),
-                pltpu.VMEM((bins * size, width), jnp.bfloat16),
                 pltpu.VMEM((size, width), jnp.float32),
             ],
         ),
         out_shape=[
             jax.ShapeDtypeStruct((count, size, width), jnp.float32),
+            jax.ShapeDtypeStruct((count, size, width), jnp.bfloat16),
             jax.ShapeDtypeStruct((count, size, width), jnp.float32),
             jax.ShapeDtypeStruct((end_rows, width), jnp.bfloat16),
         ],
@@ -263,11 +271,12 @@
 
 
 def back_kernel(
-    _, base_in, drive_in, base_out, drive_out, entering, decay, out_weight, gain, gate, upper, lower,
-    result, state, held,
+    mixed_in, normed_in, drive_in, mixed_out, normed_out, drive_out, entering, rates, out_weight, skip, gain,
+    gate, upper, lower, result, state, held,
 ):
     step = pl.program_id(0)
-    bins, inner, _ = base_in.shape
+    bins, inner = BACK_BINS, mixed_in.shape[1]
+    count = mixed_in.shape[0]
     tokens = result.shape[2]
 
     @pl.when(step == 0)
@@ -275,14 +284,21 @@
         state[...] = entering[...].astype(jnp.float32)
 
     for b in range(bins):
-        rate = decay[pl.ds(step * bins + b, 1), :]
+        rate = rates[pl.ds(step * bins + b, 1), :]
+        scale = rates[pl.ds(count + step * bins + b, 1), :]
         for start, drive in ((0, drive_in), (inner, drive_out)):
             stop = start + drive.shape[1]
-            value = rate * state[start:stop, :] + drive[b]
+            value = rate * state[start:stop, :] + scale * drive[step * bins + b]
             state[start:stop, :] = value
             held[b * tokens + start : b * tokens + stop, :] = value.astype(jnp.bfloat16)
+    skip_row = skip[...]
     base = jnp.concatenate(
-        [ref[b] for b in range(bins) for ref in (base_in, base_out)], axis=0
+        [
+            mixed[step * bins + b] + skip_row * normed[step * bins + b].astype(jnp.float32)
+            for b in range(bins)
+            for mixed, normed in ((mixed_in, normed_in), (mixed_out, normed_out))
+        ],
+        axis=0,
     )
     rows = base.shape[0]
     width = base.shape[-1]
@@ -312,23 +328,18 @@
         result[b, 0, edge + inner :, :] = done[at + inner + edge : at + tokens]
 
 
-def back(where, base_in, drive_in, base_out, drive_out, entering, decay, out_weight, gain, gate, upper, lower):
-    count, inner, width = base_in.shape
-    outer = base_out.shape[1]
+def back(inner_parts, outer_parts, *others):
+    count, inner, width = inner_parts[0].shape
+    outer = outer_parts[0].shape[1]
     bins = BACK_BINS
     tokens = inner + outer
-    blocks = [by_bin((bins, size, width)) for size in (inner, inner, outer, outer)]
+    whole = pl.BlockSpec(memory_space=pltpu.VMEM)
     return pl.pallas_call(
         back_kernel,
         grid_spec=pltpu.PrefetchScalarGridSpec(
-            num_scalar_prefetch=1,
+            num_scalar_prefetch=0,
             grid=(count // bins,),
-            in_specs=[
-                *blocks,
-                fixed(entering.shape),
-                pl.BlockSpec((count, width), lambda i, where: (where[0], 0)),
-                fixed(out_weight.shape), fixed(gain.shape), fixed(gate.shape), fixed(upper.shape), fixed(lower.shape),
-            ],
+            in_specs=[whole] * (6 + len(others)),
             out_specs=by_bin((bins, 1, tokens, width)),
             scratch_shapes=[
                 pltpu.VMEM((tokens, width), jnp.float32),
@@ -338,7 +349,7 @@
         out_shape=jax.ShapeDtypeStruct((count, 1, tokens, width), jnp.bfloat16),
         name="back",
         compiler_params=pltpu.CompilerParams(vmem_limit_bytes=32 << 20),
-    )(where, base_in, drive_in, base_out, drive_out, entering, decay, out_weight, gain, gate, upper, lower)
+    )(*inner_parts, *outer_parts, *others)
 
 
 def prefix_kernel(slots, decay, result):
@@ -376,19 +387,19 @@
     odd = ((lax.axis_index("space") + BCOLS // 2) % 2).astype(jnp.int32).reshape(1)
     gain_row, skip_row = gain_in.reshape(1, width), skip_gain.reshape(1, width)
     near_edge, far_edge, first_row, last_row, held, *shared = pack(
-        where, odd, events, mix_weight, gain_row, skip_row, in_weight, decay
+        where, odd, events, mix_weight, gain_row, in_weight, decay
     )
     far = lax.ppermute(far_edge, "space", neighbour_pairs(count, lambda c: (0, 1 if c % 2 else -1)))
     near = lax.ppermute(near_edge, "space", neighbour_pairs(count, lambda c: (0, -1 if c % 2 else 1)))
     down, up = rim(odd, near, far, first_row, last_row)
     top = lax.ppermute(down, "space", neighbour_pairs(count, lambda c: (1, 0)))
     bottom = lax.ppermute(up, "space", neighbour_pairs(count, lambda c: (-1, 0)))
-    base_in, drive_in, end_in = front(INNER, False, odd, held, near, far, (), *shared, None)
-    base_out, drive_out, ends = front(OUTER, True, odd, held, near, far, (top, bottom), *shared, end_in)
+    *inner_parts, end_in = front(INNER, False, odd, held, near, far, (), *shared, None)
+    *outer_parts, ends = front(OUTER, True, odd, held, near, far, (top, bottom), *shared, end_in)
     slots = lax.all_to_all(ends.reshape(peers, tokens_dev // peers, width), "tm", 0, 0)
     entering = lax.all_to_all(prefix(slots, decay), "tm", 0, 0).reshape(tokens_dev, width)
     return back(
-        where, base_in, drive_in, base_out, drive_out, entering, decay, out_weight,
+        inner_parts, outer_parts, entering, shared[2], out_weight, skip_row,
         feedforward_norm_gain.reshape(1, width), gate_weight, up_weight, down_weight,
     )
 

time: 64.1 us -> 63.1 us (0.984)
  Pallas kernels: 18.4 us -> 17.4 us
    pallas_call x2, Pallas kernels: 6.51 us -> 5.3 us  [front(): pl.pallas_call(functools.partial(front_kernel, rows, outer), grid_spec=pl...]
where the time goes in v1:
time: 63.1 us; the launch traced here: 62.9 us
  blocking collectives  31.4 us (50%)
  Pallas kernels  17.4 us (28%)
  starting transfers between devices  10.9 us (17%)
  waiting for transfers between devices  3.02 us (5%)
    all_to_all x1, blocking collectives, local(): lax.all_to_all(ends.reshape(peers, tokens_dev // peers, width), 'tm', 0, 0)  19.8 us
    all_to_all x1, blocking collectives, local(): lax.all_to_all(prefix(slots, decay), 'tm', 0, 0).reshape(tokens_dev, width)  11.6 us
    pallas_call x1, Pallas kernels, back(): pl.pallas_call(back_kernel, grid_spec=pltpu.PrefetchScalarGridSpec(num_sc...  9.87 us
    ppermute x1, starting transfers between devices, local(): lax.ppermute(far_edge, 'space', neighbour_pairs(count, lambda c: (0, 1 if...  5.99 us
    pallas_call x2, Pallas kernels, front(): pl.pallas_call(functools.partial(front_kernel, rows, outer), grid_spec=pl...  5.3 us
    ppermute x1, waiting for transfers between devices, local(): lax.ppermute(far_edge, 'space', neighbour_pairs(count, lambda c: (0, 1 if...  3.01 us
    ppermute x1, starting transfers between devices, local(): lax.ppermute(up, 'space', neighbour_pairs(count, lambda c: (-1, 0)))  2.66 us
    ppermute x1, starting transfers between devices, local(): lax.ppermute(near_edge, 'space', neighbour_pairs(count, lambda c: (0, -1...  2.2 us
  transfers between devices with their start and end apart: 4, of which 1 were waited for; matrix products, arithmetic and copies ran while one was open for 0% of the time, Pallas kernels for 7%

profile of v1, /device:TPU:1, one launch (start us, length us, event | category | flops | bytes accessed | tf_op | source)
XLA Modules:
  0.0 62.9 jit_solution(10647596655873190931)
XLA Ops:
  0.0 2.1 %pack.1 = (bf16[16,16,256]{2,1,0:T(8,128)(2,1)S(1)}, bf16[16,16,256]{2,1,0:T(8,128)(2,1)S(1)}, bf16[16,16,256]{2,1,0:T(8,128)(2,1)S(1)}, bf16[16,16,256]{2,1,0:T...) custom-call(s32[1]{0:T(128)} %bitcast.1._, ...), custom_call_target="tpu_custom_call" | custom-call | tf_op jit(solution)/shard_map/pack/pallas_call | solution.py:88
  2.1 2.2 %collective-permute-start = (bf16[16,16,256]{2,1,0:T(8,128)(2,1)S(1)}, bf16[16,16,256]{2,1,0:T(8,128)(2,1)S(1)}, u32[]{:S(2)}, u32[]{:S(2)}) collective-permute-start(bf16[16,16,256]{2,1,0:T(8,128)(2,1)S(1)} %get-tuple-element.24), channel_id=1, source_target_pairs={{0,1},{1,0},{2,3},{3,2},{4,5},{5,4},{6,7},{7,6},{8,9},{9,8},{10,11... | collective-permute-start | bytes 393224 | tf_op jit(solution)/shard_map/ppermute | solution.py:393
  4.3 6.0 %collective-permute-start.1 = (bf16[16,16,256]{2,1,0:T(8,128)(2,1)S(1)}, bf16[16,16,256]{2,1,0:T(8,128)(2,1)S(1)}, u32[]{:S(2)}, u32[]{:S(2)}) collective-permute-start(bf16[16,16,256]{2,1,0:T(8,128)(2,1)S(1)} %get-tuple-element.25), channel_id=1, source_target_pairs={{0,15},{3,4},{4,3},{7,8},{8,7},{11,12},{12,11},{15,0},{16,31},{19,... | collective-permute-start | bytes 393224 | tf_op jit(solution)/shard_map/ppermute | solution.py:392
  10.3 0.0 collective-permute-done.refs_2_.near
  10.3 3.0 %collective-permute-done.1.refs_3_.far = bf16[16,16,256]{2,1,0:T(8,128)(2,1)S(1)} collective-permute-done((bf16[16,16,256]{2,1,0:T(8,128)(2,1)S(1)}, bf16[16,16,256]{2,1,0:T(8,128)(2,1)S(1)}, u32[]{:S(2)}, u32[]{:S(2)}) %collective-permute-start.1) | collective-permute-done | bytes 131104 | tf_op jit(solution)/shard_map/ppermute | solution.py:392
  13.3 0.1 rim.1
  13.4 0.1 collective-permute-start.2
  13.5 2.7 %collective-permute-start.3 = (bf16[16,24,256]{2,1,0:T(8,128)(2,1)S(1)}, bf16[16,24,256]{2,1,0:T(8,128)(2,1)S(1)}, u32[]{:S(2)}, u32[]{:S(2)}) collective-permute-start(bf16[16,24,256]{2,1,0:T(8,128)(2,1)S(1)} %get-tuple-element.35), channel_id=1, source_target_pairs={{0,12},{1,13},{2,14},{3,15},{4,0},{5,1},{6,2},{7,3},{8,4},{9,5},{1... | collective-permute-start | bytes 589832 | tf_op jit(solution)/shard_map/ppermute | solution.py:396
  16.2 4.2 %front_inner.1 = (f32[16,224,256]{2,1,0:T(8,128)S(1)}, bf16[16,224,256]{2,1,0:T(8,128)(2,1)S(1)}, f32[16,224,256]{2,1,0:T(8,128)S(1)}, bf16[224,256]{1,0:T(8,128)(2,1)S(1)}) custom-call(s32[1]{0:T(128)} %bitcast.odd.refs_0_, bf16[16,1,256,256]{3,2,1,0:T(8,128)(2,1)S(1)} %get-tuple-element.23.refs_1_, ...), custom_call_target="tpu_custom_call" | custom-call | flops 506462208 | bytes 7340032 | tf_op jit(solution)/shard_map/front_inner/pallas_call | solution.py:246
  20.4 0.0 copy-start
  20.4 0.0 copy-start.1
  20.4 0.0 copy-start.2
  20.4 0.0 copy-start.3
  20.4 0.0 copy-start.4
  20.4 0.0 copy-start.5
  20.5 0.0 copy-start.6
  20.5 0.0 collective-permute-done.2.refs_4_
  20.5 0.0 collective-permute-done.3.refs_5_
  20.5 1.1 %front_outer.1 = (f32[16,32,256]{2,1,0:T(8,128)S(1)}, bf16[16,32,256]{2,1,0:T(8,128)(2,1)S(1)}, f32[16,32,256]{2,1,0:T(8,128)S(1)}, bf16[256,256]{1,0:T(8,128)(2,1)S(1)}) custom-call(s32[1]{0:T(128)} %bitcast.odd.refs_0_, bf16[16,1,256,256]{3,2,1,0:T(8,128)(2,1)S(1)} %get-tuple-element.23.refs_1_, ...), custom_call_target="tpu_custom_call" | custom-call | flops 72351744 | bytes 7340032 | tf_op jit(solution)/shard_map/front_outer/pallas_call | solution.py:246
  21.6 19.8 %all_to_all.10.slots = bf16[16,16,256]{2,1,0:T(8,128)(2,1)S(1)} all-to-all(bf16[16,16,256]{2,1,0:T(8,128)(2,1)S(1)} %bitcast.8), channel_id=1, replica_groups=mesh['tm'=16,'space'=16] {'tm'}, dimensions={0} | all-to-all | bytes 262144 | tf_op jit(solution)/shard_map/all_to_all | solution.py:399
  41.4 0.0 copy-done
  41.4 0.1 prefix.1
  41.5 11.6 %all_to_all.11 = bf16[16,16,256]{2,1,0:T(8,128)(2,1)S(1)} all-to-all(bf16[16,16,256]{2,1,0:T(8,128)(2,1)S(1)} %prefix.1), channel_id=1, replica_groups=mesh['tm'=16,'space'=16] {'tm'}, dimensions={0} | all-to-all | bytes 262144 | tf_op jit(solution)/shard_map/all_to_all | solution.py:400
  53.0 0.0 copy-done.1
  53.0 0.0 copy-done.2
  53.0 0.0 copy-done.3
  53.0 0.0 copy-done.4
  53.0 0.0 copy-done.5
  53.0 0.0 copy-done.6
  53.1 9.9 %back.1 = bf16[16,1,256,256]{3,2,1,0:T(8,128)(2,1)} custom-call(f32[16,224,256]{2,1,0:T(8,128)S(1)} %get-tuple-element.29.mixed_in, bf16[16,224,256]{2,1,0:T(8,128)(2,1)S(1)} %get-tuple-element.30.normed_in, f32[16,224,256]{2,1,0:T(8,128)S(1)} %get-tuple-element.31.drive_in, f32[16,32,256]{2,1,0:T(8,128)S(1)} %get-tuple-element.37.mixed_out, ...), custom_call_target="tpu_custom_call" | custom-call | tf_op jit(solution)/shard_map/back/pallas_call | solution.py:337
Async XLA Ops:
  2.1 8.2 %collective-permute-start = (bf16[16,16,256]{2,1,0:T(8,128)(2,1)S(1)}, bf16[16,16,256]{2,1,0:T(8,128)(2,1)S(1)}, u32[]{:S(2)}, u32[]{:S(2)}) collective-permute-start(bf16[16,16,256]{2,1,0:T(8,128)(2,1)S(1)} %get-tuple-element.24), channel_id=1, source_target_pairs={{0,1},{1,0},{2,3},{3,2},{4,5},{5,4},{6,7},{7,6},{8,9},{9,8},{10,11... | collective-permute-start | bytes 393224 | tf_op jit(solution)/shard_map/ppermute | solution.py:393
  4.3 9.0 %collective-permute-start.1 = (bf16[16,16,256]{2,1,0:T(8,128)(2,1)S(1)}, bf16[16,16,256]{2,1,0:T(8,128)(2,1)S(1)}, u32[]{:S(2)}, u32[]{:S(2)}) collective-permute-start(bf16[16,16,256]{2,1,0:T(8,128)(2,1)S(1)} %get-tuple-element.25), channel_id=1, source_target_pairs={{0,15},{3,4},{4,3},{7,8},{8,7},{11,12},{12,11},{15,0},{16,31},{19,... | collective-permute-start | bytes 393224 | tf_op jit(solution)/shard_map/ppermute | solution.py:392
  13.4 7.1 %collective-permute-start.2 = (bf16[16,24,256]{2,1,0:T(8,128)(2,1)S(1)}, bf16[16,24,256]{2,1,0:T(8,128)(2,1)S(1)}, u32[]{:S(2)}, u32[]{:S(2)}) collective-permute-start(bf16[16,24,256]{2,1,0:T(8,128)(2,1)S(1)} %get-tuple-element.34), channel_id=1, source_target_pairs={{0,4},{1,5},{2,6},{3,7},{4,8},{5,9},{6,10},{7,11},{8,12},{9,13},{1... | collective-permute-start | bytes 589832 | tf_op jit(solution)/shard_map/ppermute | solution.py:395
  13.5 7.0 %collective-permute-start.3 = (bf16[16,24,256]{2,1,0:T(8,128)(2,1)S(1)}, bf16[16,24,256]{2,1,0:T(8,128)(2,1)S(1)}, u32[]{:S(2)}, u32[]{:S(2)}) collective-permute-start(bf16[16,24,256]{2,1,0:T(8,128)(2,1)S(1)} %get-tuple-element.35), channel_id=1, source_target_pairs={{0,12},{1,13},{2,14},{3,15},{4,0},{5,1},{6,2},{7,3},{8,4},{9,5},{1... | collective-permute-start | bytes 589832 | tf_op jit(solution)/shard_map/ppermute | solution.py:396
  20.4 21.0 %copy-start = (f32[256,256]{1,0:T(8,128)S(1)}, f32[256,256]{1,0:T(8,128)}, u32[]{:S(2)}) copy-start(f32[256,256]{1,0:T(8,128)} %decay.1) | copy-start | bytes 786436
  20.4 32.6 %copy-start.1 = (bf16[256,1024]{1,0:T(8,128)(2,1)S(1)}, bf16[256,1024]{1,0:T(8,128)(2,1)}, u32[]{:S(2)}) copy-start(bf16[256,1024]{1,0:T(8,128)(2,1)} %gate.1) | copy-start | bytes 1572868
  20.4 32.6 %copy-start.2 = (bf16[256,1024]{1,0:T(8,128)(2,1)S(1)}, bf16[256,1024]{1,0:T(8,128)(2,1)}, u32[]{:S(2)}) copy-start(bf16[256,1024]{1,0:T(8,128)(2,1)} %upper.1) | copy-start | bytes 1572868
  20.4 32.6 %copy-start.3 = (bf16[1024,256]{1,0:T(8,128)(2,1)S(1)}, bf16[1024,256]{1,0:T(8,128)(2,1)}, u32[]{:S(2)}) copy-start(bf16[1024,256]{1,0:T(8,128)(2,1)} %lower.1) | copy-start | bytes 1572868
  20.4 32.6 %copy-start.4 = (bf16[256,256]{1,0:T(8,128)(2,1)S(1)}, bf16[256,256]{1,0:T(8,128)(2,1)}, u32[]{:S(2)}) copy-start(bf16[256,256]{1,0:T(8,128)(2,1)} %out_weight.1) | copy-start | bytes 393220
  20.4 32.6 %copy-start.5 = (f32[256]{0:T(256)S(1)}, f32[256]{0:T(256)}, u32[]{:S(2)}) copy-start(f32[256]{0:T(256)} %param.16) | copy-start | bytes 3076
  20.5 32.6 %copy-start.6 = (f32[256]{0:T(256)S(1)}, f32[256]{0:T(256)}, u32[]{:S(2)}) copy-start(f32[256]{0:T(256)} %param.17) | copy-start | bytes 3076

commit v2 on v1

--- a/solution.py
+++ b/solution.py
@@ -272,7 +272,7 @@
 
 def back_kernel(
     mixed_in, normed_in, drive_in, mixed_out, normed_out, drive_out, entering, rates, out_weight, skip, gain,
-    gate, upper, lower, result, state, held,
+    gate, upper, lower, result, state, held, halved,
 ):
     step = pl.program_id(0)
     bins, inner = BACK_BINS, mixed_in.shape[1]
@@ -282,6 +282,7 @@
     @pl.when(step == 0)
     def _():
         state[...] = entering[...].astype(jnp.float32)
+        halved[...] = (gate[...].astype(jnp.float32) * 0.5).astype(jnp.bfloat16)
 
     for b in range(bins):
         rate = rates[pl.ds(step * bins + b, 1), :]
@@ -302,7 +303,7 @@
     )
     rows = base.shape[0]
     width = base.shape[-1]
-    split = [slice(k * rows // 2, (k + 1) * rows // 2) for k in range(2)]
+    split = [slice(k * rows // 4, (k + 1) * rows // 4) for k in range(4)]
 
     def product(left, right):
         return jnp.concatenate(
@@ -315,7 +316,7 @@
     total = resid
     for n in range(gate.shape[-1] // width):
         part = slice(n * width, (n + 1) * width)
-        opened = 0.5 * jnp.dot(hidden, gate[:, part], preferred_element_type=jnp.float32)
+        opened = jnp.dot(hidden, halved[:, part], preferred_element_type=jnp.float32)
         raised = jnp.dot(hidden, upper[:, part], preferred_element_type=jnp.float32)
         gated = ((opened + opened * jnp.tanh(opened)) * raised).astype(jnp.bfloat16)
         total = total + product(gated, lower[part, :])
@@ -344,6 +345,7 @@
             scratch_shapes=[
                 pltpu.VMEM((tokens, width), jnp.float32),
                 pltpu.VMEM((bins * tokens, width), jnp.bfloat16),
+                pltpu.VMEM(others[5].shape, jnp.bfloat16),
             ],
         ),
         out_shape=jax.ShapeDtypeStruct((count, 1, tokens, width), jnp.bfloat16),

time: 63.1 us -> 63.1 us (level)
  no operation moved by 1% of the time
where the time goes in v2:
time: 63.1 us; the launch traced here: 62.9 us
  blocking collectives  31.4 us (50%)
  Pallas kernels  17.3 us (27%)
  starting transfers between devices  10.9 us (17%)
  waiting for transfers between devices  3.02 us (5%)
    all_to_all x1, blocking collectives, local(): lax.all_to_all(ends.reshape(peers, tokens_dev // peers, width), 'tm', 0, 0)  19.8 us
    all_to_all x1, blocking collectives, local(): lax.all_to_all(prefix(slots, decay), 'tm', 0, 0).reshape(tokens_dev, width)  11.6 us
    pallas_call x1, Pallas kernels, back(): pl.pallas_call(back_kernel, grid_spec=pltpu.PrefetchScalarGridSpec(num_sc...  9.81 us
    ppermute x1, starting transfers between devices, local(): lax.ppermute(far_edge, 'space', neighbour_pairs(count, lambda c: (0, 1 if...  5.99 us
    pallas_call x2, Pallas kernels, front(): pl.pallas_call(functools.partial(front_kernel, rows, outer), grid_spec=pl...  5.3 us
    ppermute x1, waiting for transfers between devices, local(): lax.ppermute(far_edge, 'space', neighbour_pairs(count, lambda c: (0, 1 if...  3.01 us
    ppermute x1, starting transfers between devices, local(): lax.ppermute(up, 'space', neighbour_pairs(count, lambda c: (-1, 0)))  2.66 us
    ppermute x1, starting transfers between devices, local(): lax.ppermute(near_edge, 'space', neighbour_pairs(count, lambda c: (0, -1...  2.2 us
  transfers between devices with their start and end apart: 4, of which 1 were waited for; matrix products, arithmetic and copies ran while one was open for 0% of the time, Pallas kernels for 7%

profile of v2, /device:TPU:1, one launch (start us, length us, event | category | flops | bytes accessed | tf_op | source)
XLA Modules:
  0.0 62.9 jit_solution(7539320603631013638)
XLA Ops:
  0.0 2.1 %pack.1 = (bf16[16,16,256]{2,1,0:T(8,128)(2,1)S(1)}, bf16[16,16,256]{2,1,0:T(8,128)(2,1)S(1)}, bf16[16,16,256]{2,1,0:T(8,128)(2,1)S(1)}, bf16[16,16,256]{2,1,0:T...) custom-call(s32[1]{0:T(128)} %bitcast.1._, ...), custom_call_target="tpu_custom_call" | custom-call | tf_op jit(solution)/shard_map/pack/pallas_call | solution.py:88
  2.1 2.2 %collective-permute-start = (bf16[16,16,256]{2,1,0:T(8,128)(2,1)S(1)}, bf16[16,16,256]{2,1,0:T(8,128)(2,1)S(1)}, u32[]{:S(2)}, u32[]{:S(2)}) collective-permute-start(bf16[16,16,256]{2,1,0:T(8,128)(2,1)S(1)} %get-tuple-element.24), channel_id=1, source_target_pairs={{0,1},{1,0},{2,3},{3,2},{4,5},{5,4},{6,7},{7,6},{8,9},{9,8},{10,11... | collective-permute-start | bytes 393224 | tf_op jit(solution)/shard_map/ppermute | solution.py:395
  4.3 6.0 %collective-permute-start.1 = (bf16[16,16,256]{2,1,0:T(8,128)(2,1)S(1)}, bf16[16,16,256]{2,1,0:T(8,128)(2,1)S(1)}, u32[]{:S(2)}, u32[]{:S(2)}) collective-permute-start(bf16[16,16,256]{2,1,0:T(8,128)(2,1)S(1)} %get-tuple-element.25), channel_id=1, source_target_pairs={{0,15},{3,4},{4,3},{7,8},{8,7},{11,12},{12,11},{15,0},{16,31},{19,... | collective-permute-start | bytes 393224 | tf_op jit(solution)/shard_map/ppermute | solution.py:394
  10.3 0.0 collective-permute-done.refs_2_.near
  10.3 3.0 %collective-permute-done.1.refs_3_.far = bf16[16,16,256]{2,1,0:T(8,128)(2,1)S(1)} collective-permute-done((bf16[16,16,256]{2,1,0:T(8,128)(2,1)S(1)}, bf16[16,16,256]{2,1,0:T(8,128)(2,1)S(1)}, u32[]{:S(2)}, u32[]{:S(2)}) %collective-permute-start.1) | collective-permute-done | bytes 131104 | tf_op jit(solution)/shard_map/ppermute | solution.py:394
  13.3 0.1 rim.1
  13.4 0.1 collective-permute-start.2
  13.5 2.7 %collective-permute-start.3 = (bf16[16,24,256]{2,1,0:T(8,128)(2,1)S(1)}, bf16[16,24,256]{2,1,0:T(8,128)(2,1)S(1)}, u32[]{:S(2)}, u32[]{:S(2)}) collective-permute-start(bf16[16,24,256]{2,1,0:T(8,128)(2,1)S(1)} %get-tuple-element.35), channel_id=1, source_target_pairs={{0,12},{1,13},{2,14},{3,15},{4,0},{5,1},{6,2},{7,3},{8,4},{9,5},{1... | collective-permute-start | bytes 589832 | tf_op jit(solution)/shard_map/ppermute | solution.py:398
  16.2 4.2 %front_inner.1 = (f32[16,224,256]{2,1,0:T(8,128)S(1)}, bf16[16,224,256]{2,1,0:T(8,128)(2,1)S(1)}, f32[16,224,256]{2,1,0:T(8,128)S(1)}, bf16[224,256]{1,0:T(8,128)(2,1)S(1)}) custom-call(s32[1]{0:T(128)} %bitcast.odd.refs_0_, bf16[16,1,256,256]{3,2,1,0:T(8,128)(2,1)S(1)} %get-tuple-element.23.refs_1_, ...), custom_call_target="tpu_custom_call" | custom-call | flops 506462208 | bytes 7340032 | tf_op jit(solution)/shard_map/front_inner/pallas_call | solution.py:246
  20.4 0.0 copy-start
  20.4 0.0 copy-start.1
  20.4 0.0 copy-start.2
  20.4 0.0 copy-start.3
  20.4 0.0 copy-start.4
  20.4 0.0 copy-start.5
  20.5 0.0 copy-start.6
  20.5 0.0 collective-permute-done.2.refs_4_
  20.5 0.0 collective-permute-done.3.refs_5_
  20.5 1.1 %front_outer.1 = (f32[16,32,256]{2,1,0:T(8,128)S(1)}, bf16[16,32,256]{2,1,0:T(8,128)(2,1)S(1)}, f32[16,32,256]{2,1,0:T(8,128)S(1)}, bf16[256,256]{1,0:T(8,128)(2,1)S(1)}) custom-call(s32[1]{0:T(128)} %bitcast.odd.refs_0_, bf16[16,1,256,256]{3,2,1,0:T(8,128)(2,1)S(1)} %get-tuple-element.23.refs_1_, ...), custom_call_target="tpu_custom_call" | custom-call | flops 72351744 | bytes 7340032 | tf_op jit(solution)/shard_map/front_outer/pallas_call | solution.py:246
  21.6 19.8 %all_to_all.10.slots = bf16[16,16,256]{2,1,0:T(8,128)(2,1)S(1)} all-to-all(bf16[16,16,256]{2,1,0:T(8,128)(2,1)S(1)} %bitcast.8), channel_id=1, replica_groups=mesh['tm'=16,'space'=16] {'tm'}, dimensions={0} | all-to-all | bytes 262144 | tf_op jit(solution)/shard_map/all_to_all | solution.py:401
  41.4 0.0 copy-done
  41.4 0.1 prefix.1
  41.5 11.6 %all_to_all.11 = bf16[16,16,256]{2,1,0:T(8,128)(2,1)S(1)} all-to-all(bf16[16,16,256]{2,1,0:T(8,128)(2,1)S(1)} %prefix.1), channel_id=1, replica_groups=mesh['tm'=16,'space'=16] {'tm'}, dimensions={0} | all-to-all | bytes 262144 | tf_op jit(solution)/shard_map/all_to_all | solution.py:402
  53.0 0.0 copy-done.1
  53.0 0.0 copy-done.2
  53.0 0.0 copy-done.3
  53.0 0.0 copy-done.4
  53.0 0.0 copy-done.5
  53.0 0.0 copy-done.6
  53.1 9.8 %back.1 = bf16[16,1,256,256]{3,2,1,0:T(8,128)(2,1)} custom-call(f32[16,224,256]{2,1,0:T(8,128)S(1)} %get-tuple-element.29.mixed_in, bf16[16,224,256]{2,1,0:T(8,128)(2,1)S(1)} %get-tuple-element.30.normed_in, f32[16,224,256]{2,1,0:T(8,128)S(1)} %get-tuple-element.31.drive_in, f32[16,32,256]{2,1,0:T(8,128)S(1)} %get-tuple-element.37.mixed_out, ...), custom_call_target="tpu_custom_call" | custom-call | tf_op jit(solution)/shard_map/back/pallas_call | solution.py:338
Async XLA Ops:
  2.1 8.2 %collective-permute-start = (bf16[16,16,256]{2,1,0:T(8,128)(2,1)S(1)}, bf16[16,16,256]{2,1,0:T(8,128)(2,1)S(1)}, u32[]{:S(2)}, u32[]{:S(2)}) collective-permute-start(bf16[16,16,256]{2,1,0:T(8,128)(2,1)S(1)} %get-tuple-element.24), channel_id=1, source_target_pairs={{0,1},{1,0},{2,3},{3,2},{4,5},{5,4},{6,7},{7,6},{8,9},{9,8},{10,11... | collective-permute-start | bytes 393224 | tf_op jit(solution)/shard_map/ppermute | solution.py:395
  4.3 9.0 %collective-permute-start.1 = (bf16[16,16,256]{2,1,0:T(8,128)(2,1)S(1)}, bf16[16,16,256]{2,1,0:T(8,128)(2,1)S(1)}, u32[]{:S(2)}, u32[]{:S(2)}) collective-permute-start(bf16[16,16,256]{2,1,0:T(8,128)(2,1)S(1)} %get-tuple-element.25), channel_id=1, source_target_pairs={{0,15},{3,4},{4,3},{7,8},{8,7},{11,12},{12,11},{15,0},{16,31},{19,... | collective-permute-start | bytes 393224 | tf_op jit(solution)/shard_map/ppermute | solution.py:394
  13.4 7.1 %collective-permute-start.2 = (bf16[16,24,256]{2,1,0:T(8,128)(2,1)S(1)}, bf16[16,24,256]{2,1,0:T(8,128)(2,1)S(1)}, u32[]{:S(2)}, u32[]{:S(2)}) collective-permute-start(bf16[16,24,256]{2,1,0:T(8,128)(2,1)S(1)} %get-tuple-element.34), channel_id=1, source_target_pairs={{0,4},{1,5},{2,6},{3,7},{4,8},{5,9},{6,10},{7,11},{8,12},{9,13},{1... | collective-permute-start | bytes 589832 | tf_op jit(solution)/shard_map/ppermute | solution.py:397
  13.5 7.0 %collective-permute-start.3 = (bf16[16,24,256]{2,1,0:T(8,128)(2,1)S(1)}, bf16[16,24,256]{2,1,0:T(8,128)(2,1)S(1)}, u32[]{:S(2)}, u32[]{:S(2)}) collective-permute-start(bf16[16,24,256]{2,1,0:T(8,128)(2,1)S(1)} %get-tuple-element.35), channel_id=1, source_target_pairs={{0,12},{1,13},{2,14},{3,15},{4,0},{5,1},{6,2},{7,3},{8,4},{9,5},{1... | collective-permute-start | bytes 589832 | tf_op jit(solution)/shard_map/ppermute | solution.py:398
  20.4 21.0 %copy-start = (f32[256,256]{1,0:T(8,128)S(1)}, f32[256,256]{1,0:T(8,128)}, u32[]{:S(2)}) copy-start(f32[256,256]{1,0:T(8,128)} %decay.1) | copy-start | bytes 786436
  20.4 32.6 %copy-start.1 = (bf16[256,1024]{1,0:T(8,128)(2,1)S(1)}, bf16[256,1024]{1,0:T(8,128)(2,1)}, u32[]{:S(2)}) copy-start(bf16[256,1024]{1,0:T(8,128)(2,1)} %gate.1) | copy-start | bytes 1572868
  20.4 32.6 %copy-start.2 = (bf16[256,1024]{1,0:T(8,128)(2,1)S(1)}, bf16[256,1024]{1,0:T(8,128)(2,1)}, u32[]{:S(2)}) copy-start(bf16[256,1024]{1,0:T(8,128)(2,1)} %upper.1) | copy-start | bytes 1572868
  20.4 32.6 %copy-start.3 = (bf16[1024,256]{1,0:T(8,128)(2,1)S(1)}, bf16[1024,256]{1,0:T(8,128)(2,1)}, u32[]{:S(2)}) copy-start(bf16[1024,256]{1,0:T(8,128)(2,1)} %lower.1) | copy-start | bytes 1572868
  20.4 32.6 %copy-start.4 = (bf16[256,256]{1,0:T(8,128)(2,1)S(1)}, bf16[256,256]{1,0:T(8,128)(2,1)}, u32[]{:S(2)}) copy-start(bf16[256,256]{1,0:T(8,128)(2,1)} %out_weight.1) | copy-start | bytes 393220
  20.4 32.6 %copy-start.5 = (f32[256]{0:T(256)S(1)}, f32[256]{0:T(256)}, u32[]{:S(2)}) copy-start(f32[256]{0:T(256)} %param.16) | copy-start | bytes 3076
  20.5 32.6 %copy-start.6 = (f32[256]{0:T(256)S(1)}, f32[256]{0:T(256)}, u32[]{:S(2)}) copy-start(f32[256]{0:T(256)} %param.17) | copy-start | bytes 3076
